TPU v7x, 512 devices: a whole 4x8x8 slice. The times are simulated.
512 devices in a mesh: dp: 8 (over y), expert: 64 (over x, z, core).
Axes of the slice: x: 4, y: 8, z: 8, core: 2. Of those that a mesh axis runs over, the one named last changes fastest.
Arguments:
- tokens: bfloat16 [8192, 4096], P('expert', 'dp'), may hold values from -6 to 6
- cotangent: bfloat16 [8192, 4096], P('expert', 'dp'), may hold values from -6 to 6
- expert_ids: int32 [8192, 6], P('expert'), may hold values from 0 to 63, all different within a row; in each aligned block of 128 rows (0 to 127, 128 to 255, ...) at most 14 rows name the same one
- route_probs: bfloat16 [8192, 6], P('expert'), may hold values from 0.049804688 to 1
- w_gate: bfloat16 [64, 4096, 768], P('expert', 'dp'), may hold values from -0.09375 to 0.09375
- w_up: bfloat16 [64, 4096, 768], P('expert', 'dp'), may hold values from -0.09375 to 0.09375
- w_down: bfloat16 [64, 768, 4096], P('expert', None, 'dp'), may hold values from -0.09375 to 0.09375
Outputs:
- grad_tokens: bfloat16 [8192, 4096], P('expert', 'dp')
- grad_gate: bfloat16 [64, 4096, 768], P('expert', 'dp')
- grad_up: bfloat16 [64, 4096, 768], P('expert', 'dp')
- grad_down: bfloat16 [64, 768, 4096], P('expert', None, 'dp')
- d_probs: bfloat16 [8192, 6], P('expert')
Inputs may be any that keep to these rules, and one draw needn't show every extreme that they name: `expert_ids`: each row names 6 different experts and every expert is named by some row; in each aligned block of 128 rows no expert is named by more than 14 rows, a bound that some block reaches.
All inputs are finite; a program needn't handle non-finite values.
Results may differ from a plain program's by a relative error of at most 0.024.
Values may be sent and summed in bfloat16 or wider, within the bound.
A program may use at most 64 MiB of HBM per device.

v0:
```python
import jax
import jax.numpy as jnp
from jax import lax
from jax.sharding import PartitionSpec as P


def silu_parts(gate_sum):
    logistic = jax.nn.sigmoid(gate_sum)
    return (gate_sum * logistic, logistic * (1.0 + gate_sum * (1.0 - logistic)))


def local_step(gate_sum, up_sum, grad_h, gate_probs):
    activated, derivative = silu_parts(gate_sum)
    hidden_f = lax.optimization_barrier((activated * up_sum).astype(jnp.bfloat16)).astype(
        jnp.float32
    )
    prob_grad = jnp.sum(hidden_f * grad_h, axis=1).astype(jnp.bfloat16)
    scaled = gate_probs[:, None] * grad_h
    d_gate = (scaled * up_sum * derivative).astype(jnp.bfloat16)
    d_up = (scaled * activated).astype(jnp.bfloat16)
    h_scaled = (gate_probs[:, None] * hidden_f).astype(jnp.bfloat16)
    return (h_scaled, d_gate, d_up, prob_grad)


def contract_rows(a, b):
    return lax.dot_general(a, b, (((0,), (0,)), ((), ())), preferred_element_type=jnp.float32)


def contract_columns(a, b):
    return lax.dot_general(a, b, (((1,), (1,)), ((), ())), preferred_element_type=jnp.float32)


def exchange(rows):
    return lax.all_to_all(rows, "expert", split_axis=0, concat_axis=0, tiled=True)


def local(tokens, cotangent, expert_ids, route_probs, w_gate, w_up, w_down):
    expert_count = lax.axis_size("expert")
    token_count, columns = tokens.shape
    fanout = expert_ids.shape[1]
    capacity = max(2, 7 * token_count * fanout // (6 * expert_count))
    gate_w, up_w, down_w = (w_gate[0], w_up[0], w_down[0])
    experts = jnp.arange(expert_count, dtype=jnp.int32)
    hits = expert_ids.T[:, None, :] == experts[None, :, None]
    chosen = jnp.any(hits, axis=0)
    order = jnp.arange(token_count, dtype=jnp.int32)
    before = (order[:, None] < order[None, :]).astype(jnp.bfloat16)
    earlier = jnp.dot(chosen.astype(jnp.bfloat16), before, preferred_element_type=jnp.float32)
    slot_of = jnp.where(chosen, earlier.astype(jnp.int32), -1)
    probs_f = route_probs.astype(jnp.float32)
    prob_of = jnp.sum(jnp.where(hits, probs_f.T[:, None, :], 0.0), axis=0)
    both = jnp.concatenate([tokens, cotangent], axis=1)
    all_slots = jnp.arange(capacity, dtype=jnp.int32)
    match = slot_of[:, None, :] == all_slots[None, :, None]
    padded = jnp.arange(capacity + 2, dtype=jnp.int32)
    pick = (slot_of[:, None, :] == padded[None, :, None]).astype(jnp.bfloat16)
    rows = (
        jnp.dot(
            pick.reshape(expert_count * (capacity + 2), token_count),
            both,
            preferred_element_type=jnp.float32,
        )
        .astype(jnp.bfloat16)
        .reshape(expert_count, capacity + 2, 2 * columns)
    )
    sent_p = jnp.sum(jnp.where(match, prob_of[:, None, :], 0.0), axis=2).astype(jnp.bfloat16)
    p_row = jnp.pad(sent_p, ((0, 0), (0, 2 * columns - capacity)))
    rows = jnp.where((padded == capacity)[None, :, None], p_row[:, None, :], rows)
    received = exchange(rows)
    rows_all = expert_count * capacity
    gate_probs = received[:, capacity, :capacity].reshape(rows_all).astype(jnp.float32)
    got = received[:, :capacity].reshape(rows_all, 2 * columns)
    x_rows, dy_rows = (got[:, :columns], got[:, columns:])
    parts = (
        jnp.dot(x_rows, gate_w, preferred_element_type=jnp.float32),
        jnp.dot(x_rows, up_w, preferred_element_type=jnp.float32),
        contract_columns(dy_rows, down_w),
    )
    gate_sum, up_sum, grad_h = (
        lax.psum(v.astype(jnp.bfloat16), "dp").astype(jnp.float32) for v in parts
    )
    h_scaled, d_gate, d_up, prob_grad = local_step(gate_sum, up_sum, grad_h, gate_probs)
    dx_rows = contract_columns(d_gate, gate_w) + contract_columns(d_up, up_w)
    dx_rows = dx_rows.astype(jnp.bfloat16).reshape(expert_count, capacity, columns)
    prob_row = jnp.pad(prob_grad.reshape(expert_count, capacity), ((0, 0), (0, columns - capacity)))
    back = exchange(jnp.concatenate([dx_rows, prob_row[:, None, :]], axis=1))
    grad_gate = contract_rows(x_rows, d_gate)
    grad_up = contract_rows(x_rows, d_up)
    grad_down = contract_rows(h_scaled, dy_rows)
    total = contract_rows(
        match.astype(jnp.bfloat16).reshape(rows_all, token_count),
        back[:, :capacity].reshape(rows_all, columns),
    )
    back_p = back[:, capacity, :capacity].astype(jnp.float32)
    back_of = jnp.sum(jnp.where(match, back_p[:, :, None], 0.0), axis=1)
    d_probs = jnp.sum(jnp.where(hits, back_of[None], 0.0), axis=1).T.astype(jnp.bfloat16)
    return (
        total.astype(jnp.bfloat16),
        grad_gate.astype(jnp.bfloat16)[None],
        grad_up.astype(jnp.bfloat16)[None],
        grad_down.astype(jnp.bfloat16)[None],
        d_probs,
    )


def solution(mesh):
    in_specs = (
        P("expert", "dp"),
        P("expert", "dp"),
        P("expert", None),
        P("expert", None),
        P("expert", "dp", None),
        P("expert", "dp", None),
        P("expert", None, "dp"),
    )
    out_specs = (
        P("expert", "dp"),
        P("expert", "dp", None),
        P("expert", "dp", None),
        P("expert", None, "dp"),
        P("expert", None),
    )
    return jax.shard_map(local, mesh=mesh, in_specs=in_specs, out_specs=out_specs, check_vma=False)
```

profile of v0, /device:TPU:1, one launch (start us, length us, event | category | flops | bytes accessed | tf_op | source)
XLA Modules:
  0.0 261.2 jit_solution(15965414682091480196)
XLA Ops:
  7.2 0.0 copy-start
  7.2 0.0 all-reduce.5.cloned.1.call-start
  7.2 0.7 convert_bitcast_fusion
  8.0 0.7 fusion.38
  8.7 0.1 fusion.20
  8.8 0.7 select_reduce_fusion.3
  9.6 0.2 select_reduce_fusion.1
  9.8 0.1 copy.28
  9.9 0.1 eq.63
  10.0 0.2 bitcast_compare_fusion
  10.2 1.7 convolution_convert_fusion
  11.9 0.0 copy-done.9
  11.9 0.2 broadcast_select_fusion
  12.1 65.8 %all_to_all.10 = bf16[64,16,1024]{2,1,0:T(8,128)(2,1)S(1)} all-to-all(bf16[64,16,1024]{2,1,0:T(8,128)(2,1)S(1)} %broadcast_select_fusion), channel_id=1, replica_groups=mesh['dp'=8,'expert'=64] {'expert'}, dimensions={0} | all-to-all | bytes 4194304 | tf_op jit(solution)/shard_map/all_to_all | solution.py:34
  78.0 1.5 reshape.52
  79.5 0.0 copy-done
  79.5 3.4 %convolution_convert_fusion.1 = bf16[896,768]{1,0:T(8,128)(2,1)} fusion(bf16[1,512,768]{2,1,0:T(8,128)(2,1)S(1)} %copy-done, bf16[896,1024]{1,0:T(8,128)(2,1)} %reshape.52), kind=kOutput, calls=%fused_computation.23 | convolution fusion | flops 705331200 | bytes 3080192 | tf_op jit(solution)/shard_map/dot_general | solution.py:75
  82.8 0.0 copy-done.2
  82.9 2.0 convolution_convert_fusion.2
  84.9 2.0 convolution_convert_fusion.3
  86.9 0.0 all-reduce.5.cloned.1.call-update
  86.9 0.1 fusion.39
  87.0 0.1 reshape.54
  87.2 0.0 copy-start.12
  87.2 109.1 %all-reduce.5.cloned.1.call-done = (bf16[896,768]{1,0:T(8,128)(2,1)}, bf16[896,768]{1,0:T(8,128)(2,1)}, bf16[896,768]{1,0:T(8,128)(2,1)}) async-done(((bf16[896,768]{1,0:T(8,128)(2,1)}, bf16[896,768]{1,0:T(8,128)(2,1)}, bf16[896,768]{1,0:T(8,128)(2,1)}), (bf16[896,768]{1,0:T(8,128)(2,1)}, bf16[896,768]{1,0:T(8,128)(2,1)}, bf16[896,768]{1,0:T(8,128)(2,1)})) %all-reduce.5.cloned.1.call-update) | async-done | bytes 4128784 | tf_op jit(solution)/shard_map/psum | solution.py:80
  196.3 4.5 %fusion.1 = (bf16[896,768]{1,0:T(8,128)(2,1)}, bf16[896,768]{1,0:T(8,128)(2,1)S(1)}, bf16[896,768]{1,0:T(8,128)(2,1)S(1)}) fusion(bf16[896,768]{1,0:T(8,128)(2,1)} %get-tuple-element.5, f32[896]{0:T(1024)S(1)} %reshape.54, bf16[896,768]{1,0:T(8,128)(2,1)} %get-tuple-element.7, bf16[896,768]{1,0:T(8,128)(2,1)} %get-tuple-element.6), kind=kLoop, calls=%fused_computation.9 | loop fusion | flops 13074432 | bytes 8261120 | tf_op jit(solution)/shard_map/convert_element_type | solution.py:20
  200.8 1.0 fusion.5
  201.8 0.8 convert_element_type.116
  202.7 0.8 copy.24
  203.4 0.9 fusion.24
  204.3 0.4 copy-done.6
  204.8 0.2 copy-done.16
  205.0 1.8 add_convert_fusion
  206.8 1.4 reshape.53
  208.2 0.0 copy-done.8
  208.2 1.3 pad_maximum_fusion
  209.5 11.5 %all-to-all-start.1 = ((bf16[64,15,512]{2,1,0:T(8,128)(2,1)}), bf16[64,15,512]{2,1,0:T(8,128)(2,1)}, u32[]{:S(2)}, u32[]{:S(2)}) async-start(bf16[64,15,512]{2,1,0:T(8,128)(2,1)} %pad_maximum_fusion), calls=%async_computation.1 | async-start | bytes 2097152 | tf_op jit(solution)/shard_map/all_to_all | solution.py:34
  221.1 3.2 %fusion.15 = bf16[1,512,768]{2,1,0:T(8,128)(2,1)} fusion(bf16[896,768]{1,0:T(8,128)(2,1)S(1)} %copy-done.7, bf16[896,1024]{1,0:T(8,128)(2,1)} %reshape.52), kind=kOutput, calls=%fused_computation.31 | convolution fusion | flops 705036288 | bytes 3080192 | tf_op jit(solution)/shard_map/dot_general | solution.py:26
  224.3 1.9 fusion.14
  226.3 2.0 fusion.16
  228.3 21.2 %all-to-all-done.1 = bf16[64,15,512]{2,1,0:T(8,128)(2,1)} async-done(((bf16[64,15,512]{2,1,0:T(8,128)(2,1)}), bf16[64,15,512]{2,1,0:T(8,128)(2,1)}, u32[]{:S(2)}, u32[]{:S(2)}) %all-to-all-start.1) | async-done | bytes 983072 | tf_op jit(solution)/shard_map/all_to_all | solution.py:34
  249.5 0.9 slice_convert_fusion
  250.4 0.1 copy.26
  250.5 0.0 copy-done.10
  250.5 0.2 select_reduce_fusion
  250.7 3.0 %fusion.19 = bf16[128,512]{1,0:T(8,128)(2,1)} fusion(bf16[64,14,512]{2,1,0:T(8,128)(2,1)} %bitcast.42, s32[64,128]{1,0:T(8,128)S(1)} %copy-done.10), kind=kOutput, calls=%fused_computation.34 | convolution fusion | flops 117620736 | bytes 1081344 | tf_op jit(solution)/shard_map/dot_general | solution.py:26
  253.7 0.0 copy-done.11
  253.7 0.6 select_reduce_fusion.2
  (28 shorter events, 0.1 us)
Async XLA Ops:
  7.2 72.3 %copy-start = (bf16[1,512,768]{2,1,0:T(8,128)(2,1)S(1)}, bf16[1,512,768]{2,1,0:T(8,128)(2,1)}, u32[]{:S(2)}) copy-start(bf16[1,512,768]{2,1,0:T(8,128)(2,1)} %param.11) | copy-start | bytes 2359300
  7.2 189.1 %all-reduce.5.cloned.1.call-start = ((), (), s32[]{:S(2)}) async-start(), calls=%async_computation.2 | async-start | bytes 8257536 | tf_op jit(solution)/shard_map/psum | solution.py:80
  8.8 3.0 %copy-start.9 = (s32[64,128]{1,0:T(8,128)}, s32[64,128]{1,0:T(8,128)S(1)}, u32[]{:S(2)}) copy-start(s32[64,128]{1,0:T(8,128)S(1)} %fusion.20) | copy-start | bytes 98308
  79.5 3.4 %copy-start.2 = (bf16[896,1024]{1,0:T(8,128)(2,1)S(1)}, bf16[896,1024]{1,0:T(8,128)(2,1)}, u32[]{:S(2)}) copy-start(bf16[896,1024]{1,0:T(8,128)(2,1)} %reshape.52) | copy-start | bytes 5505028
  79.5 3.4 %copy-start.15 = (bf16[1,512,768]{2,1,0:T(8,128)(2,1)S(1)}, bf16[1,512,768]{2,1,0:T(8,128)(2,1)}, u32[]{:S(2)}) copy-start(bf16[1,512,768]{2,1,0:T(8,128)(2,1)} %param.12) | copy-start | bytes 2359300
  82.9 2.0 copy-start.14
  87.2 113.6 %copy-start.12 = (f32[896]{0:T(1024)}, f32[896]{0:T(1024)S(1)}, u32[]{:S(2)}) copy-start(f32[896]{0:T(1024)S(1)} %reshape.54) | copy-start | bytes 10756
  196.3 4.5 %copy-start.1 = (bf16[896,768]{1,0:T(8,128)(2,1)S(1)}, bf16[896,768]{1,0:T(8,128)(2,1)}, u32[]{:S(2)}) copy-start(bf16[896,768]{1,0:T(8,128)(2,1)} %get-tuple-element.5) | copy-start | bytes 4128772
  200.8 3.5 %copy-start.4 = (bf16[896,768]{1,0:T(8,128)(2,1)}, bf16[896,768]{1,0:T(8,128)(2,1)S(1)}, u32[]{:S(2)}) copy-start(bf16[896,768]{1,0:T(8,128)(2,1)S(1)} %get-tuple-element.9) | copy-start | bytes 4128772
  203.4 1.3 copy-start.6
  203.4 1.5 copy-start.16
  206.8 1.4 copy-start.8
  209.5 11.5 %copy-start.7 = (bf16[896,768]{1,0:T(8,128)(2,1)S(1)}, bf16[896,768]{1,0:T(8,128)(2,1)}, u32[]{:S(2)}) copy-start(bf16[896,768]{1,0:T(8,128)(2,1)} %get-tuple-element.8) | copy-start | bytes 4128772
  209.5 40.0 %all-to-all-start.1 = ((bf16[64,15,512]{2,1,0:T(8,128)(2,1)}), bf16[64,15,512]{2,1,0:T(8,128)(2,1)}, u32[]{:S(2)}, u32[]{:S(2)}) async-start(bf16[64,15,512]{2,1,0:T(8,128)(2,1)} %pad_maximum_fusion), calls=%async_computation.1 | async-start | bytes 2097152 | tf_op jit(solution)/shard_map/all_to_all | solution.py:34
  221.1 3.3 %copy-start.3 = (bf16[896,1024]{1,0:T(8,128)(2,1)S(1)}, bf16[896,1024]{1,0:T(8,128)(2,1)}, u32[]{:S(2)}) copy-start(bf16[896,1024]{1,0:T(8,128)(2,1)} %reshape.52) | copy-start | bytes 5505028
  221.1 3.3 %copy-start.5 = (bf16[896,768]{1,0:T(8,128)(2,1)S(1)}, bf16[896,768]{1,0:T(8,128)(2,1)}, u32[]{:S(2)}) copy-start(bf16[896,768]{1,0:T(8,128)(2,1)} %copy-done.4) | copy-start | bytes 4128772
  224.3 1.9 copy-start.13
  226.3 24.2 %copy-start.10 = (s32[64,128]{1,0:T(8,128)S(1)}, s32[64,128]{1,0:T(8,128)}, u32[]{:S(2)}) copy-start(s32[64,128]{1,0:T(8,128)} %copy-done.9) | copy-start | bytes 98308
  226.3 27.5 %copy-start.11 = (s32[128,6]{0,1:T(8,128)S(1)}, s32[128,6]{0,1:T(8,128)}, u32[]{:S(2)}) copy-start(s32[128,6]{0,1:T(8,128)} %param.9) | copy-start | bytes 9220
Sparse Core Ops, SparseCore 0:
  87.0 109.2 all-reduce.4
where the time goes:
time: 262 us; the launch traced here: 261 us
  waiting for transfers between devices  130 us (50%)
  blocking collectives  65.8 us (25%)
  matrix products  22.1 us (8%)
  between operations  14.2 us (5%)
  starting transfers between devices  11.6 us (4%)
  other arithmetic  11.5 us (4%)
  local copies, waits for them, and re-layouts  5.61 us (2%)
    psum x1, waiting for transfers between devices, local(): lax.psum(v.astype(jnp.bfloat16), 'dp').astype(jnp.float32)  109 us
    all_to_all x1, blocking collectives, exchange(): lax.all_to_all(rows, 'expert', split_axis=0, concat_axis=0, tiled=True)  65.8 us
    all_to_all x1, waiting for transfers between devices, exchange(): lax.all_to_all(rows, 'expert', split_axis=0, concat_axis=0, tiled=True)  21.2 us
    all_to_all x1, starting transfers between devices, exchange(): lax.all_to_all(rows, 'expert', split_axis=0, concat_axis=0, tiled=True)  11.5 us
    dot_general x4, matrix products, contract_rows(): lax.dot_general(a, b, (((0,), (0,)), ((), ())), preferred_element_type=jn...  10.2 us
  transfers between devices with their start and end apart: 2, of which 2 were waited for; matrix products, arithmetic and copies ran while one was open for 3% of the time, Pallas kernels for 0%

commit v1 on v0

--- a/solution.py
+++ b/solution.py
@@ -77,7 +77,8 @@
         contract_columns(dy_rows, down_w),
     )
     gate_sum, up_sum, grad_h = (
-        lax.psum(v.astype(jnp.bfloat16), "dp").astype(jnp.float32) for v in parts
+        jnp.sum(lax.all_gather(v.astype(jnp.bfloat16), "dp"), axis=0).astype(jnp.float32)
+        for v in parts
     )
     h_scaled, d_gate, d_up, prob_grad = local_step(gate_sum, up_sum, grad_h, gate_probs)
     dx_rows = contract_columns(d_gate, gate_w) + contract_columns(d_up, up_w)

time: 262 us -> 513 us (1.96)
  waiting for transfers between devices: 130 us -> 362 us
  other arithmetic: 11.5 us -> 31 us
    all_gather x0 -> x3, waiting for transfers between devices: none -> 341 us  [local(): lax.all_gather(v.astype(jnp.bfloat16), 'dp')]
    psum x1 -> x0, waiting for transfers between devices: 109 us -> none  [local(): lax.psum(v.astype(jnp.bfloat16), 'dp').astype(jnp.float32)]
    reduce_sum x0 -> x3, other arithmetic: none -> 20.2 us  [local(): jnp.sum(lax.all_gather(v.astype(jnp.bfloat16), 'dp'), axis=0)]
  transfers between devices with their start and end apart: 2 -> 4, of which waited for: 2 -> 4; matrix products, arithmetic and copies ran while one was open for 3% -> 5% of each run, Pallas kernels for 0% -> 0%
where the time goes in v1:
time: 513 us; the launch traced here: 512 us
  waiting for transfers between devices  362 us (71%)
  blocking collectives  65.8 us (13%)
  other arithmetic  31 us (6%)
  matrix products  23.9 us (5%)
  between operations  13.9 us (3%)
  starting transfers between devices  11.8 us (2%)
    all_gather x3, waiting for transfers between devices, local(): lax.all_gather(v.astype(jnp.bfloat16), 'dp')  341 us
    all_to_all x1, blocking collectives, exchange(): lax.all_to_all(rows, 'expert', split_axis=0, concat_axis=0, tiled=True)  65.8 us
    all_to_all x1, waiting for transfers between devices, exchange(): lax.all_to_all(rows, 'expert', split_axis=0, concat_axis=0, tiled=True)  21.1 us
    reduce_sum x3, other arithmetic, local(): jnp.sum(lax.all_gather(v.astype(jnp.bfloat16), 'dp'), axis=0)  20.2 us
    all_to_all x1, starting transfers between devices, exchange(): lax.all_to_all(rows, 'expert', split_axis=0, concat_axis=0, tiled=True)  11.5 us
    dot_general x4, matrix products, contract_rows(): lax.dot_general(a, b, (((0,), (0,)), ((), ())), preferred_element_type=jn...  10.3 us
  transfers between devices with their start and end apart: 4, of which 4 were waited for; matrix products, arithmetic and copies ran while one was open for 5% of the time, Pallas kernels for 0%

profile of v1, /device:TPU:1, one launch (start us, length us, event | category | flops | bytes accessed | tf_op | source)
XLA Modules:
  0.0 512.5 jit_solution(8196883079974947065)
XLA Ops:
  7.2 0.0 all-gather.11.cloned.1.call-start
  7.2 0.7 convert_bitcast_fusion
  8.0 0.7 fusion.38
  8.7 0.1 fusion.20
  8.8 0.7 select_reduce_fusion.3
  9.6 0.2 select_reduce_fusion.1
  9.8 0.1 copy.28
  9.9 0.1 eq.63
  10.0 0.2 bitcast_compare_fusion
  10.2 1.7 convolution_convert_fusion
  11.9 0.2 broadcast_select_fusion
  12.1 65.8 %all_to_all.10 = bf16[64,16,1024]{2,1,0:T(8,128)(2,1)S(1)} all-to-all(bf16[64,16,1024]{2,1,0:T(8,128)(2,1)S(1)} %broadcast_select_fusion), channel_id=1, replica_groups=mesh['dp'=8,'expert'=64] {'expert'}, dimensions={0} | all-to-all | bytes 4194304 | tf_op jit(solution)/shard_map/all_to_all | solution.py:34
  78.0 1.5 reshape.52
  79.5 3.2 convolution_convert_fusion.1
  82.6 0.0 all-gather.11.cloned.1.call-update
  82.6 0.0 all-gather.9.cloned.1.call-start
  82.7 3.4 convolution_convert_fusion.2
  86.1 0.2 all-gather.7.cloned.1.call-start
  86.3 3.4 convolution_convert_fusion.3
  89.7 0.1 fusion.39
  89.9 0.1 reshape.54
  90.0 110.1 %all-gather.11.cloned.1.call-done = bf16[7168,768]{1,0:T(8,128)(2,1)} async-done(((bf16[896,768]{1,0:T(8,128)(2,1)}), bf16[7168,768]{1,0:T(8,128)(2,1)}) %all-gather.11.cloned.1.call-update) | async-done | bytes 11010064 | tf_op jit(solution)/shard_map/all_gather | solution.py:80
  200.1 6.5 %reduce_sum.85 = bf16[896,768]{1,0:T(8,128)(2,1)S(1)} reduce(bf16[8,896,768]{2,1,0:T(8,128)(2,1)} %bitcast.46, bf16[]{:T(256)} %constant.14.clone.1), dimensions={0}, to_apply=%region_5.6 | reduce | flops 4816896 | bytes 12386306 | tf_op jit(solution)/shard_map/reduce_sum | solution.py:80
  206.6 115.6 %all-gather.9.cloned.1.call-done = bf16[7168,768]{1,0:T(8,128)(2,1)} async-done(((bf16[896,768]{1,0:T(8,128)(2,1)}), bf16[7168,768]{1,0:T(8,128)(2,1)}) %all-gather.9.cloned.1.call-update) | async-done | bytes 11010064 | tf_op jit(solution)/shard_map/all_gather | solution.py:80
  322.2 7.2 %reduce_sum.84 = bf16[896,768]{1,0:T(8,128)(2,1)} reduce(bf16[8,896,768]{2,1,0:T(8,128)(2,1)} %bitcast.47, bf16[]{:T(256)} %constant.14.clone.1), dimensions={0}, to_apply=%region_4.5 | reduce | flops 4816896 | bytes 12386306 | tf_op jit(solution)/shard_map/reduce_sum | solution.py:80
  329.4 115.0 %all-gather.7.cloned.1.call-done = bf16[7168,768]{1,0:T(8,128)(2,1)} async-done(((bf16[896,768]{1,0:T(8,128)(2,1)}), bf16[7168,768]{1,0:T(8,128)(2,1)}) %all-gather.7.cloned.1.call-update) | async-done | bytes 11010064 | tf_op jit(solution)/shard_map/all_gather | solution.py:80
  444.3 6.5 %reduce_sum.83 = bf16[896,768]{1,0:T(8,128)(2,1)S(1)} reduce(bf16[8,896,768]{2,1,0:T(8,128)(2,1)} %bitcast.48, bf16[]{:T(256)} %constant.14.clone.1), dimensions={0}, to_apply=%region_3.4 | reduce | flops 4816896 | bytes 12386306 | tf_op jit(solution)/shard_map/reduce_sum | solution.py:80
  450.9 4.3 fusion.1
  455.2 1.1 copy-done.1
  456.3 0.4 fusion.5
  456.8 0.1 convert_element_type.122
  456.9 0.1 copy.24
  457.1 0.9 fusion.24
  458.0 0.4 copy-done.6
  458.4 0.2 copy-done.10
  458.6 0.9 add_convert_fusion
  459.5 0.3 reshape.53
  459.8 1.4 pad_maximum_fusion
  461.1 11.5 %all-to-all-start.1 = ((bf16[64,15,512]{2,1,0:T(8,128)(2,1)}), bf16[64,15,512]{2,1,0:T(8,128)(2,1)}, u32[]{:S(2)}, u32[]{:S(2)}) async-start(bf16[64,15,512]{2,1,0:T(8,128)(2,1)} %pad_maximum_fusion), calls=%async_computation.1 | async-start | bytes 2097152 | tf_op jit(solution)/shard_map/all_to_all | solution.py:34
  472.7 3.4 fusion.15
  476.0 1.9 fusion.14
  478.0 2.0 fusion.16
  480.0 21.1 %all-to-all-done.1 = bf16[64,15,512]{2,1,0:T(8,128)(2,1)} async-done(((bf16[64,15,512]{2,1,0:T(8,128)(2,1)}), bf16[64,15,512]{2,1,0:T(8,128)(2,1)}, u32[]{:S(2)}, u32[]{:S(2)}) %all-to-all-start.1) | async-done | bytes 983072 | tf_op jit(solution)/shard_map/all_to_all | solution.py:34
  501.1 0.9 slice_convert_fusion
  502.0 0.1 copy.26
  502.1 0.2 select_reduce_fusion
  502.3 3.0 fusion.19
  505.3 0.6 select_reduce_fusion.2
  (25 shorter events, 0.1 us)
Async XLA Ops:
  7.2 72.3 %copy-start = (bf16[1,512,768]{2,1,0:T(8,128)(2,1)S(1)}, bf16[1,512,768]{2,1,0:T(8,128)(2,1)}, u32[]{:S(2)}) copy-start(bf16[1,512,768]{2,1,0:T(8,128)(2,1)} %param.11) | copy-start | bytes 2359300
  7.2 192.9 %all-gather.11.cloned.1.call-start = ((), (), s32[]{:S(2)}) async-start(), calls=%async_computation.4 | async-start | bytes 12386304 | tf_op jit(solution)/shard_map/all_gather | solution.py:80
  8.8 3.0 copy-start.7
  82.6 239.6 %all-gather.9.cloned.1.call-start = ((), (), s32[]{:S(2)}) async-start(), calls=%async_computation.3 | async-start | bytes 12386304 | tf_op jit(solution)/shard_map/all_gather | solution.py:80
  86.1 358.2 %all-gather.7.cloned.1.call-start = ((), (), s32[]{:S(2)}) async-start(), calls=%async_computation.2 | async-start | bytes 12386304 | tf_op jit(solution)/shard_map/all_gather | solution.py:80
  455.2 1.1 copy-start.1
  455.2 1.8 copy-start.4
  457.0 1.3 copy-start.6
  457.0 1.5 copy-start.10
  461.1 11.5 %copy-start.3 = (bf16[896,1024]{1,0:T(8,128)(2,1)S(1)}, bf16[896,1024]{1,0:T(8,128)(2,1)}, u32[]{:S(2)}) copy-start(bf16[896,1024]{1,0:T(8,128)(2,1)} %reshape.52) | copy-start | bytes 5505028
  461.1 40.0 %all-to-all-start.1 = ((bf16[64,15,512]{2,1,0:T(8,128)(2,1)}), bf16[64,15,512]{2,1,0:T(8,128)(2,1)}, u32[]{:S(2)}, u32[]{:S(2)}) async-start(bf16[64,15,512]{2,1,0:T(8,128)(2,1)} %pad_maximum_fusion), calls=%async_computation.1 | async-start | bytes 2097152 | tf_op jit(solution)/shard_map/all_to_all | solution.py:34
  472.7 3.4 copy-start.5
  476.0 1.9 copy-start.2
  478.0 24.1 %copy-start.8 = (s32[64,128]{1,0:T(8,128)S(1)}, s32[64,128]{1,0:T(8,128)}, u32[]{:S(2)}) copy-start(s32[64,128]{1,0:T(8,128)} %copy-done.7) | copy-start | bytes 98308
  478.0 27.4 %copy-start.9 = (s32[128,6]{0,1:T(8,128)S(1)}, s32[128,6]{0,1:T(8,128)}, u32[]{:S(2)}) copy-start(s32[128,6]{0,1:T(8,128)} %param.9) | copy-start | bytes 9220
Sparse Core Ops, SparseCore 0:
  82.8 117.2 all-gather.10
  202.2 119.9 all-gather.8
  324.3 119.9 all-gather.6
